TPU v7x, 32 devices: a whole 2x2x4 slice. The times are simulated.
32 devices in a mesh: dp: 4 (over y, x), seq: 8 (over z, core).
Axes of the slice: x: 2, y: 2, z: 4, core: 2. Of those that a mesh axis runs over, the one named last changes fastest.
Arguments:
- queries: bfloat16 [16, 4096, 128], P(None, ('dp', 'seq')), parts along dimension 1, may hold values from -6 to 6
- key_pairs: bfloat16 [16, 4096, 256], P(None, ('dp', 'seq')), parts along dimension 1, may hold values from -6 to 6
- value_pairs: bfloat16 [16, 4096, 256], P(None, ('dp', 'seq')), parts along dimension 1, may hold values from -6 to 6
- strengths: float32 [16, 8192], P(None, ('dp', 'seq')), parts along dimension 1, may hold values from 0.002 to 1.99
- decays: float32 [16, 4096], P(None, ('dp', 'seq')), parts along dimension 1, may hold values from 0 to 1, as said below
- conv_query: float32 [16, 4, 128], replicated, may hold values from -1.5 to 1.5
- conv_key: float32 [16, 4, 256], replicated, may hold values from -1.5 to 1.5
- conv_value: float32 [16, 4, 256], replicated, may hold values from -1.5 to 1.5
- doc_lengths: int32 [32], P('dp'), parts along dimension 0, may hold values from 1 to 512, 1024 in all
Outputs:
- readout: bfloat16 [16, 4096, 128], P(None, ('dp', 'seq')), parts along dimension 1
There are 4 independent parts, one for each index of `dp`. A program takes and returns all parts, laid end to end along the dimension named above; an argument that names none is the same for every part. Nothing has to cross between parts.
Inputs may be any that keep to these rules, and one draw needn't show every extreme that they name: `doc_lengths`: they sum to 1024, and the longest document has exactly 512 tokens. Every gate exp(-decays) lies between 0.36 and 1.
All inputs are finite; a program needn't handle non-finite values.
Results may differ from a plain program's by a relative error of at most 0.0062.
Values may be sent and summed in bfloat16 or wider, within the bound.
A program may use at most 320 MiB of HBM per device.

v0:
```python
import jax
import jax.numpy as jnp
from jax import lax
from jax.sharding import PartitionSpec as P

highest = lax.Precision.HIGHEST


def passed_along(block, axis, distance):
    devices = range(lax.axis_size(axis))
    route = [(i - distance, i) for i in devices if i - distance in devices]
    return lax.ppermute(block, axis, route)


def entering(part, axis, combine, identity):
    place = lax.axis_index(axis)
    gathered = lax.all_gather(part, axis)
    state = jnp.zeros_like(part) + jnp.asarray(identity, part.dtype)

    def one(hop, state):
        return combine(state, lax.dynamic_index_in_dim(gathered, hop, 0, False))

    return lax.fori_loop(0, place, one, state)


def doc_starts(doc_lengths):
    ending = jnp.cumsum(doc_lengths)
    return ending - doc_lengths


def since_start(starts, offset, span_len):
    position = offset + jnp.arange(span_len, dtype=jnp.int32)
    reached = starts[None, :] <= position[:, None]
    latest = jnp.max(jnp.where(reached, starts[None, :], 0), axis=1)
    return position - latest


def short_conv(values, border, kernel, since):
    length = values.shape[1]
    border_len = border.shape[1]
    extended = jnp.concatenate([border, values], axis=1).astype(jnp.float32)
    summed = kernel[:, 0:1, :] * extended[:, border_len:, :]
    for lag_step in range(1, border_len + 1):
        shifted = extended[:, border_len - lag_step : border_len - lag_step + length, :]
        usable = (since >= lag_step)[None, :, None]
        summed = summed + jnp.where(usable, kernel[:, lag_step : lag_step + 1, :] * shifted, 0.0)
    return jax.nn.silu(summed)


def unit_rows(values, width):
    grouped = values.reshape(values.shape[0], -1, width)
    scale = lax.rsqrt(jnp.sum(grouped * grouped, axis=-1, keepdims=True) + 1e-06)
    return (grouped * scale).astype(jnp.bfloat16)


def prepare(
    queries,
    key_pairs,
    value_pairs,
    query_border,
    key_border,
    value_border,
    conv_query,
    conv_key,
    conv_value,
    since,
):
    heads = queries.shape[0]
    key_width = queries.shape[2]
    value_width = value_pairs.shape[2] // 2
    query_unit = unit_rows(short_conv(queries, query_border, conv_query, since), key_width)
    key_unit = unit_rows(short_conv(key_pairs, key_border, conv_key, since), key_width)
    value_unit = (
        short_conv(value_pairs, value_border, conv_value, since)
        .astype(jnp.bfloat16)
        .reshape(heads, -1, value_width)
    )
    return (query_unit, key_unit, value_unit)


def head_terms(query, keys, values, strength, decay, since):
    tokens_here = query.shape[0]
    steps = keys.shape[0]
    key_width = keys.shape[1]
    value_width = values.shape[1]
    log_gate = jnp.stack([-decay, jnp.zeros_like(decay)], axis=1).reshape(steps)
    opening = jnp.stack([since == 0, since < 0], axis=1).reshape(steps)
    running = jnp.cumsum(log_gate)
    segment = jnp.cumsum(opening.astype(jnp.int32))
    sub_index = jnp.arange(steps, dtype=jnp.int32)
    linked = (segment[:, None] == segment[None, :]) & (sub_index[:, None] > sub_index[None, :])
    log_gap = jnp.where(linked, running[:, None] - running[None, :], 0.0)
    intersection = jnp.einsum("sk,rk->sr", keys, keys, preferred_element_type=jnp.float32)
    system = jnp.eye(steps, dtype=jnp.float32) + jnp.where(
        linked, strength[:, None] * jnp.exp(log_gap) * intersection, 0.0
    )
    open_gain = jnp.where(segment == 0, jnp.exp(running), 0.0)
    keys_wide = keys.astype(jnp.float32)
    targets = jnp.concatenate(
        [
            strength[:, None] * values.astype(jnp.float32),
            (strength * open_gain)[:, None] * keys_wide,
        ],
        axis=1,
    )
    solved = jax.scipy.linalg.solve_triangular(system, targets, lower=True, unit_diagonal=True)
    end_gain = jnp.where(segment == segment[steps - 1], jnp.exp(running[steps - 1] - running), 0.0)
    weighted = keys_wide * end_gain[:, None]
    moved = jnp.einsum(
        "nr,nk->rk", solved, weighted, precision=highest, preferred_element_type=jnp.float32
    )
    transit = open_gain[steps - 1] * jnp.eye(key_width, dtype=jnp.float32) - moved[value_width:]
    carry_pair = jnp.concatenate([transit, moved[:value_width]], axis=0)
    out_rows = jnp.arange(tokens_here, dtype=jnp.int32) * 2 + 1
    out_segment = segment.reshape(tokens_here, 2)[:, 1]
    out_running = running.reshape(tokens_here, 2)[:, 1]
    reads = (out_segment[:, None] == segment[None, :]) & (out_rows[:, None] >= sub_index[None, :])
    read_gap = jnp.where(reads, out_running[:, None] - running[None, :], 0.0)
    scores = jnp.einsum("ck,nk->cn", query, keys, preferred_element_type=jnp.float32)
    mixing = jnp.where(reads, jnp.exp(read_gap) * scores, 0.0)
    gathered = jnp.dot(mixing, solved, precision=highest, preferred_element_type=jnp.float32)
    out_gain = open_gain.reshape(tokens_here, 2)[:, 1]
    correction = out_gain[:, None] * query.astype(jnp.float32) - gathered[:, value_width:]
    return (carry_pair, gathered[:, :value_width], correction)


def compose(early, late):
    key_width = late.shape[2]
    product = jnp.einsum(
        "hij,hjk->hik",
        early,
        late[:, :key_width],
        precision=highest,
        preferred_element_type=jnp.float32,
    )
    return jnp.concatenate(
        [product[:, :key_width], product[:, key_width:] + late[:, key_width:]], axis=1
    )


def body(
    queries,
    key_pairs,
    value_pairs,
    strengths,
    decays,
    conv_query,
    conv_key,
    conv_value,
    doc_lengths,
):
    heads = queries.shape[0]
    tokens_here = queries.shape[1]
    key_width = queries.shape[2]
    pair_width = key_pairs.shape[2]
    value_width = value_pairs.shape[2] // 2
    border_len = conv_query.shape[1] - 1
    offset = lax.axis_index("seq") * tokens_here
    since = since_start(doc_starts(doc_lengths), offset, tokens_here)
    tails = jnp.concatenate(
        [
            queries[:, tokens_here - border_len :],
            key_pairs[:, tokens_here - border_len :],
            value_pairs[:, tokens_here - border_len :],
        ],
        axis=2,
    )
    borders = passed_along(tails, "seq", 1)
    query_border = borders[:, :, :key_width]
    key_border = borders[:, :, key_width : key_width + pair_width]
    value_border = borders[:, :, key_width + pair_width :]
    query_unit, key_unit, value_unit = prepare(
        queries,
        key_pairs,
        value_pairs,
        query_border,
        key_border,
        value_border,
        conv_query,
        conv_key,
        conv_value,
        since,
    )

    def per_head(pieces):
        return head_terms(pieces[0], pieces[1], pieces[2], pieces[3], pieces[4], since)

    carry_pairs, local_out, correction = lax.map(
        per_head, (query_unit, key_unit, value_unit, strengths, decays)
    )
    identity = jnp.concatenate(
        [
            jnp.broadcast_to(jnp.eye(key_width, dtype=jnp.float32), (heads, key_width, key_width)),
            jnp.zeros((heads, value_width, key_width), jnp.float32),
        ],
        axis=1,
    )
    prefix_pair = entering(carry_pairs, "seq", compose, identity)
    start_state = prefix_pair[:, key_width:]
    readout = local_out + jnp.einsum(
        "hck,hvk->hcv",
        correction,
        start_state,
        precision=highest,
        preferred_element_type=jnp.float32,
    )
    return readout.astype(jnp.bfloat16)


def solution(mesh):
    in_specs = (
        P(None, ("dp", "seq"), None),
        P(None, ("dp", "seq"), None),
        P(None, ("dp", "seq"), None),
        P(None, ("dp", "seq")),
        P(None, ("dp", "seq")),
        P(),
        P(),
        P(),
        P("dp"),
    )
    out_specs = P(None, ("dp", "seq"), None)
    return jax.shard_map(body, mesh=mesh, in_specs=in_specs, out_specs=out_specs, check_vma=False)
```

profile of v0, /device:TPU:27, one launch (start us, length us, event | category | flops | bytes accessed | tf_op | source)
XLA Modules:
  0.0 883.0 jit_solution(1537010971674270713)
XLA Ops:
  18.4 4.4 multiply_convert_fusion
  28.3 618.6 %while.27 = (s32[]{:T(128)}, f32[16,256,128]{2,1,0:T(8,128)}, f32[16,128,128]{2,1,0:T(8,128)S(1)}, f32[16,128,128]{2,1,0:T(8,128)S(1)}, s32[128]{0:T(128)S(1)}, ...) while((s32[]{:T(128)}, f32[16,256,128]{2,1,0:T(8,128)}, ...), condition=%wide.region_9.10_spmd, body=%wide.region_4.9_spmd.sunk | while | flops 379391616 | bytes 4319790 | solution.py:188
  38.1 4.0 while.29
  42.1 19.7 %custom-call.9 = f32[2,128,128]{1,2,0:T(8,128)S(1)} custom-call(f32[2,128,128]{2,1,0:T(8,128)S(1)} %get-tuple-element.326), custom_call_target="InvertDiagBlocksLowerTriangular" | custom-call | tf_op jit(solution)/shard_map/while/body/eval_jaxpr/jit(_solve_triangular)/triangular_solve | solution.py:106
  76.8 4.0 while.29
  80.8 19.7 %custom-call.9 = f32[2,128,128]{1,2,0:T(8,128)S(1)} custom-call(f32[2,128,128]{2,1,0:T(8,128)S(1)} %get-tuple-element.326), custom_call_target="InvertDiagBlocksLowerTriangular" | custom-call | tf_op jit(solution)/shard_map/while/body/eval_jaxpr/jit(_solve_triangular)/triangular_solve | solution.py:106
  115.4 4.0 while.29
  119.4 19.7 %custom-call.9 = f32[2,128,128]{1,2,0:T(8,128)S(1)} custom-call(f32[2,128,128]{2,1,0:T(8,128)S(1)} %get-tuple-element.326), custom_call_target="InvertDiagBlocksLowerTriangular" | custom-call | tf_op jit(solution)/shard_map/while/body/eval_jaxpr/jit(_solve_triangular)/triangular_solve | solution.py:106
  154.1 4.0 while.29
  158.1 19.7 %custom-call.9 = f32[2,128,128]{1,2,0:T(8,128)S(1)} custom-call(f32[2,128,128]{2,1,0:T(8,128)S(1)} %get-tuple-element.326), custom_call_target="InvertDiagBlocksLowerTriangular" | custom-call | tf_op jit(solution)/shard_map/while/body/eval_jaxpr/jit(_solve_triangular)/triangular_solve | solution.py:106
  192.8 4.0 while.29
  196.8 19.7 %custom-call.9 = f32[2,128,128]{1,2,0:T(8,128)S(1)} custom-call(f32[2,128,128]{2,1,0:T(8,128)S(1)} %get-tuple-element.326), custom_call_target="InvertDiagBlocksLowerTriangular" | custom-call | tf_op jit(solution)/shard_map/while/body/eval_jaxpr/jit(_solve_triangular)/triangular_solve | solution.py:106
  231.4 4.0 while.29
  235.4 19.7 %custom-call.9 = f32[2,128,128]{1,2,0:T(8,128)S(1)} custom-call(f32[2,128,128]{2,1,0:T(8,128)S(1)} %get-tuple-element.326), custom_call_target="InvertDiagBlocksLowerTriangular" | custom-call | tf_op jit(solution)/shard_map/while/body/eval_jaxpr/jit(_solve_triangular)/triangular_solve | solution.py:106
  274.1 19.7 %custom-call.9 = f32[2,128,128]{1,2,0:T(8,128)S(1)} custom-call(f32[2,128,128]{2,1,0:T(8,128)S(1)} %get-tuple-element.326), custom_call_target="InvertDiagBlocksLowerTriangular" | custom-call | tf_op jit(solution)/shard_map/while/body/eval_jaxpr/jit(_solve_triangular)/triangular_solve | solution.py:106
  308.7 4.0 while.29
  312.7 19.7 %custom-call.9 = f32[2,128,128]{1,2,0:T(8,128)S(1)} custom-call(f32[2,128,128]{2,1,0:T(8,128)S(1)} %get-tuple-element.326), custom_call_target="InvertDiagBlocksLowerTriangular" | custom-call | tf_op jit(solution)/shard_map/while/body/eval_jaxpr/jit(_solve_triangular)/triangular_solve | solution.py:106
  351.4 19.7 %custom-call.9 = f32[2,128,128]{1,2,0:T(8,128)S(1)} custom-call(f32[2,128,128]{2,1,0:T(8,128)S(1)} %get-tuple-element.326), custom_call_target="InvertDiagBlocksLowerTriangular" | custom-call | tf_op jit(solution)/shard_map/while/body/eval_jaxpr/jit(_solve_triangular)/triangular_solve | solution.py:106
  386.1 4.0 while.29
  390.1 19.7 %custom-call.9 = f32[2,128,128]{1,2,0:T(8,128)S(1)} custom-call(f32[2,128,128]{2,1,0:T(8,128)S(1)} %get-tuple-element.326), custom_call_target="InvertDiagBlocksLowerTriangular" | custom-call | tf_op jit(solution)/shard_map/while/body/eval_jaxpr/jit(_solve_triangular)/triangular_solve | solution.py:106
  424.7 4.0 while.29
  428.7 19.7 %custom-call.9 = f32[2,128,128]{1,2,0:T(8,128)S(1)} custom-call(f32[2,128,128]{2,1,0:T(8,128)S(1)} %get-tuple-element.326), custom_call_target="InvertDiagBlocksLowerTriangular" | custom-call | tf_op jit(solution)/shard_map/while/body/eval_jaxpr/jit(_solve_triangular)/triangular_solve | solution.py:106
  467.4 19.7 %custom-call.9 = f32[2,128,128]{1,2,0:T(8,128)S(1)} custom-call(f32[2,128,128]{2,1,0:T(8,128)S(1)} %get-tuple-element.326), custom_call_target="InvertDiagBlocksLowerTriangular" | custom-call | tf_op jit(solution)/shard_map/while/body/eval_jaxpr/jit(_solve_triangular)/triangular_solve | solution.py:106
  506.0 19.7 %custom-call.9 = f32[2,128,128]{1,2,0:T(8,128)S(1)} custom-call(f32[2,128,128]{2,1,0:T(8,128)S(1)} %get-tuple-element.326), custom_call_target="InvertDiagBlocksLowerTriangular" | custom-call | tf_op jit(solution)/shard_map/while/body/eval_jaxpr/jit(_solve_triangular)/triangular_solve | solution.py:106
  540.7 4.0 while.29
  544.7 19.7 %custom-call.9 = f32[2,128,128]{1,2,0:T(8,128)S(1)} custom-call(f32[2,128,128]{2,1,0:T(8,128)S(1)} %get-tuple-element.326), custom_call_target="InvertDiagBlocksLowerTriangular" | custom-call | tf_op jit(solution)/shard_map/while/body/eval_jaxpr/jit(_solve_triangular)/triangular_solve | solution.py:106
  583.3 19.7 %custom-call.9 = f32[2,128,128]{1,2,0:T(8,128)S(1)} custom-call(f32[2,128,128]{2,1,0:T(8,128)S(1)} %get-tuple-element.326), custom_call_target="InvertDiagBlocksLowerTriangular" | custom-call | tf_op jit(solution)/shard_map/while/body/eval_jaxpr/jit(_solve_triangular)/triangular_solve | solution.py:106
  618.0 4.0 while.29
  622.0 19.7 %custom-call.9 = f32[2,128,128]{1,2,0:T(8,128)S(1)} custom-call(f32[2,128,128]{2,1,0:T(8,128)S(1)} %get-tuple-element.326), custom_call_target="InvertDiagBlocksLowerTriangular" | custom-call | tf_op jit(solution)/shard_map/while/body/eval_jaxpr/jit(_solve_triangular)/triangular_solve | solution.py:106
  648.5 149.1 %all-gather.3.cloned.1.call-done = f32[128,256,128]{2,1,0:T(8,128)} async-done(((f32[16,256,128]{2,1,0:T(8,128)}), f32[128,256,128]{2,1,0:T(8,128)}) %all-gather.3.cloned.1.call-update) | async-done | bytes 16777232 | tf_op jit(solution)/shard_map/all_gather | solution.py:17
  797.7 72.3 %while.28 = (s32[]{:T(128)}, f32[16,256,128]{1,2,0:T(8,128)}, s32[]{:T(128)}, f32[8,16,256,128]{3,2,1,0:T(8,128)}, s32[]{:T(128)}, /*index=5*/s32[]{:T(128)}, s32[]{:T(128)}) while((s32[]{:T(128)}, f32[16,256,128]{1,2,0:T(8,128)}, s32[]{:T(128)}, f32[8,16,256,128]{3,2,1,0:T(8,128)}, s32[]{:T(128)}, /*index=5*/s32[]{:T(128)}, ...), condition=%wide.region_11.12_spmd, body=%wide.region_10.11_spmd.sunk | while | flops 806092800 | bytes 23068796 | solution.py:23
  871.9 4.3 fusion.48
  (950 shorter events, 413.2 us)
Async XLA Ops:
  6.5 791.1 %all-gather.3.cloned.1.call-start = ((), (), s32[]{:S(2)}) async-start(), calls=%async_computation | async-start | bytes 18874368 | tf_op jit(solution)/shard_map/all_gather | solution.py:17
  9.1 6.0 collective-permute-start
  16.3 1.2 copy-start.1
  16.3 1.5 copy-start.2
  646.9 1.7 copy-start
Sparse Core Ops, SparseCore 0:
  647.0 150.6 all-gather.2
where the time goes:
time: 890 us; the launch traced here: 883 us
  other arithmetic  428 us (48%)
  local copies, waits for them, and re-layouts  181 us (20%)
  waiting for transfers between devices  149 us (17%)
  matrix products  106 us (12%)
  between operations  13.6 us (2%)
    another operation x48, other arithmetic, head_terms(): jax.scipy.linalg.solve_triangular(system, targets, lower=True, unit_diago...  315 us
    all_gather x1, waiting for transfers between devices, entering(): gathered = lax.all_gather(part, axis)  149 us
    another operation x274, local copies, waits for them, and re-layouts  81.1 us
    dynamic_slice x14, local copies, waits for them, and re-layouts, one(): return combine(state, lax.dynamic_index_in_dim(gathered, hop, 0, False))  35.4 us
    dot_general x7, matrix products, compose(): jnp.einsum('hij,hjk->hik', early, late[:, :key_width], precision=highest,...  24.5 us
    dot_general x16, matrix products, head_terms(): jnp.einsum('nr,nk->rk', solved, weighted, precision=highest, preferred_el...  23.9 us
    select_n x16, other arithmetic, head_terms(): jnp.where(segment == segment[steps - 1], jnp.exp(running[steps - 1] - run...  21.2 us
    dot_general x16, matrix products, head_terms(): jnp.einsum('sk,rk->sr', keys, keys, preferred_element_type=jnp.float32)  18.6 us
  transfers between devices with their start and end apart: 2, of which 1 were waited for; matrix products, arithmetic and copies ran while one was open for 1% of the time, Pallas kernels for 0%

commit v1 on v0

v1 whole, which is shorter than its diff:
```python
import functools

import jax
import jax.numpy as jnp
from jax import lax
from jax.experimental import pallas as pl
from jax.experimental.pallas import tpu as pltpu
from jax.sharding import PartitionSpec as P

MESH = pl.DeviceIdType.MESH
BF = jnp.bfloat16
F32 = jnp.float32
FAR = -1e30
GROUP = 2
NT = (((1,), (1,)), ((), ()))


def mm(a, b):
    return jnp.dot(a.astype(BF), b.astype(BF), preferred_element_type=F32)


def split(a):
    high = a.astype(BF)
    return high, (a - high.astype(F32)).astype(BF)


def mm_wide(a, b):
    a_high, a_low = split(a)
    b_high, b_low = split(b)
    return mm(a_high, b_high) + (mm(a_high, b_low) + mm(a_low, b_high))


def exact_nt(a, b):
    return lax.dot_general(
        a, b, NT, precision=lax.Precision.HIGHEST, preferred_element_type=F32
    )


def iota(shape, axis):
    return lax.broadcasted_iota(jnp.int32, shape, axis)


def kernel(
    n_seq,
    docs_ref,
    q_ref,
    k_ref,
    v_ref,
    strength_ref,
    decay_ref,
    cq_ref,
    ck_ref,
    cv_ref,
    out_ref,
    bq_ref,
    bk_ref,
    bv_ref,
    ext_ref,
    usable_ref,
    bias_l_ref,
    bias_m_ref,
    open_col_ref,
    rows_ref,
    beta_cols_ref,
    run_cols_ref,
    run_rows_ref,
    maps_ref,
    terms_ref,
    arrived_ref,
    leaving_ref,
    border_send,
    border_recv,
    state_send,
    state_recv,
):
    heads, tokens, width = q_ref.shape
    half = tokens // 2
    steps = 2 * tokens
    pairs = heads // GROUP
    me = lax.axis_index("seq")
    offset = me * tokens
    has_left = me > 0
    has_right = me < n_seq - 1
    barrier = pltpu.get_barrier_semaphore()

    @pl.when(has_left)
    def _():
        pl.semaphore_signal(barrier, inc=1, device_id={"seq": me - 1}, device_id_type=MESH)

    def border_copies(pair):
        span = pl.ds(pair * GROUP, GROUP)
        return [
            pltpu.make_async_remote_copy(
                src_ref=source.at[span, pl.ds(tokens - 16, 16), :],
                dst_ref=target.at[span],
                send_sem=border_send.at[which, pair],
                recv_sem=border_recv.at[which, pair],
                device_id={"seq": me + 1},
                device_id_type=MESH,
            )
            for which, (source, target) in enumerate(
                [(q_ref, bq_ref), (k_ref, bk_ref), (v_ref, bv_ref)]
            )
        ]

    def state_copy(head):
        return pltpu.make_async_remote_copy(
            src_ref=leaving_ref.at[head],
            dst_ref=arrived_ref.at[head],
            send_sem=state_send.at[head],
            recv_sem=state_recv.at[head],
            device_id={"seq": me + 1},
            device_id_type=MESH,
        )

    @pl.when(has_right)
    def _():
        pl.semaphore_wait(barrier, 1)

        def send(pair, carry):
            for copy in border_copies(pair):
                copy.start()
            return carry

        lax.fori_loop(0, pairs, send, 0)

    @pl.when(me == 0)
    def _():
        bq_ref[...] = jnp.zeros_like(bq_ref)
        bk_ref[...] = jnp.zeros_like(bk_ref)
        bv_ref[...] = jnp.zeros_like(bv_ref)
        arrived_ref[...] = jnp.zeros_like(arrived_ref)

    def token_of(index):
        return (index // tokens) * half + index % half

    def sub_of(index):
        return 2 * token_of(index) + (index // half) % 2

    starts = []
    total = jnp.int32(0)
    for m in range(docs_ref.shape[0]):
        starts.append(total)
        total = total + docs_ref[m]

    def latest_of(position):
        latest = jnp.zeros_like(position)
        for start in starts:
            latest = jnp.maximum(latest, jnp.where(start <= position, start, 0))
        return latest

    token_col = token_of(iota((steps, tokens), 0))
    token_row = token_of(iota((8, steps), 1))
    latest_col = latest_of(offset + token_col)
    latest_row = latest_of(offset + token_row)
    position = offset + iota((tokens, tokens), 0)
    since = position - latest_of(position)
    for lag in range(1, 4):
        usable_ref[lag - 1] = jnp.where(since >= lag, 1.0, 0.0)
    sub_col = sub_of(iota((steps, steps), 0))
    sub_row = sub_of(iota((steps, steps), 1))
    wide_latest = jnp.concatenate([latest_col, latest_col], axis=1)
    same = wide_latest == latest_row[0:1]
    bias_l_ref[...] = jnp.where(same & (sub_col > sub_row), 0.0, FAR)
    reads = jnp.where(same & (sub_col + 1 >= sub_row), 0.0, FAR)
    bias_m_ref[...] = jnp.concatenate([reads[:half], reads[tokens : tokens + half]], axis=0)
    open_col_ref[...] = jnp.where(latest_col < offset, 0.0, FAR)
    last = token_row == tokens - 1
    final = jnp.max(latest_row, axis=1, keepdims=True)
    rows_ref[0] = jnp.where(latest_row == final, 0.0, FAR)
    rows_ref[1] = jnp.where(jnp.broadcast_to(final < offset, last.shape), 0.0, FAR)

    pick = jnp.where(sub_col == iota((steps, steps), 1), 1.0, 0.0)
    beta_cols_ref[...] = exact_nt(pick, strength_ref[...])
    summed = jnp.where(iota((steps, tokens), 1) <= token_col, -1.0, 0.0)
    run_cols_ref[...] = exact_nt(summed, decay_ref[...])
    run_rows_ref[...] = exact_nt(decay_ref[...], summed)

    lane_head = iota((steps, heads), 1)
    in_half = iota((tokens, tokens), 0) % half
    apart = in_half ^ (iota((tokens, tokens), 1) % half)
    eye = jnp.where(
        iota((tokens, tokens), 0) == iota((tokens, tokens), 1), 1.0, 0.0
    )
    eye_width = jnp.where(
        iota((width, width), 0) == iota((width, width), 1), 1.0, 0.0
    )
    both = range(GROUP)

    def convolved(u, head, lane, kernel_ref, column):
        here = slice(lane, lane + width)
        summed = kernel_ref[head, 0:1, column : column + width] * ext_ref[u, 16 : 16 + tokens, here]
        for lag in range(1, 4):
            shifted = ext_ref[u, 16 - lag : 16 - lag + tokens, here]
            tap = kernel_ref[head, lag : lag + 1, column : column + width]
            summed = summed + usable_ref[lag - 1] * (tap * shifted)
        return summed / (1.0 + jnp.exp(-summed))

    def unit(rows):
        scale = lax.rsqrt(jnp.sum(rows * rows, axis=1, keepdims=True) + 1e-6)
        return (rows * scale).astype(BF)

    def arranged(first, second):
        return jnp.concatenate([first[:half], second[:half], first[half:], second[half:]], axis=0)

    def one_j(rows):
        return jnp.concatenate([rows[:half], rows[tokens : tokens + half]], axis=0)

    def local(pair):
        ids = [pair * GROUP + u for u in both]
        for u in both:
            head = ids[u]
            ext_ref[u, 0:16, 0:width] = bq_ref[head].astype(F32)
            ext_ref[u, 0:16, width : 3 * width] = bk_ref[head].astype(F32)
            ext_ref[u, 0:16, 3 * width : 5 * width] = bv_ref[head].astype(F32)
            ext_ref[u, 16 : 16 + tokens, 0:width] = q_ref[head].astype(F32)
            ext_ref[u, 16 : 16 + tokens, width : 3 * width] = k_ref[head].astype(F32)
            ext_ref[u, 16 : 16 + tokens, 3 * width : 5 * width] = v_ref[head].astype(F32)
        query = [unit(convolved(u, ids[u], 0, cq_ref, 0)) for u in both]
        keys = [
            arranged(
                unit(convolved(u, ids[u], width, ck_ref, 0)),
                unit(convolved(u, ids[u], 2 * width, ck_ref, width)),
            )
            for u in both
        ]
        values = [
            arranged(
                convolved(u, ids[u], 3 * width, cv_ref, 0).astype(BF),
                convolved(u, ids[u], 4 * width, cv_ref, width).astype(BF),
            )
            for u in both
        ]
        beta = [
            jnp.sum(jnp.where(lane_head == ids[u], beta_cols_ref[...], 0.0), axis=1, keepdims=True)
            for u in both
        ]
        run_col = [
            jnp.sum(jnp.where(lane_head == ids[u], run_cols_ref[...], 0.0), axis=1, keepdims=True)
            for u in both
        ]
        run_row = [run_rows_ref[pl.ds(ids[u], 1), :] for u in both]
        run_last = [
            jnp.sum(
                jnp.where(iota((1, steps), 1) == steps - 1, run_row[u], 0.0), axis=1, keepdims=True
            )
            for u in both
        ]
        products = [
            lax.dot_general(
                jnp.concatenate([keys[u], query[u], eye_width.astype(BF)], axis=0),
                keys[u],
                NT,
                preferred_element_type=F32,
            )
            for u in both
        ]
        system = []
        for u in both:
            top = jnp.exp(run_col[u][:tokens] - run_row[u][:, :tokens] + bias_l_ref[:tokens, :tokens])
            low = jnp.exp(run_col[u][tokens:] - run_row[u] + bias_l_ref[tokens:, :])
            top = top * (beta[u][:tokens] * products[u][:tokens, :tokens])
            low = low * (beta[u][tokens:] * products[u][tokens:steps])
            system.append((top, low[:, :tokens].astype(BF), low[:, tokens:]))
        blocks = [system[u][side] for u in both for side in (0, 2)]
        inverse = [eye - jnp.where(apart == 0, block, 0.0) for block in blocks]
        level = 1
        while level < half:
            at_level = (apart >= level) & (apart < 2 * level)
            narrow = [x.astype(BF) for x in inverse]
            inner = [
                mm(jnp.where(at_level, block, 0.0), x) for block, x in zip(blocks, narrow)
            ]
            inverse = [x - mm(n, y) for x, n, y in zip(inverse, narrow, inner)]
            level *= 2
        inverse = [x.astype(BF) for x in inverse]
        opened = [jnp.exp(run_col[u] + open_col_ref[...]) for u in both]
        targets = [
            jnp.concatenate(
                [
                    beta[u] * values[u].astype(F32),
                    (beta[u] * opened[u]) * keys[u].astype(F32),
                ],
                axis=1,
            )
            for u in both
        ]
        first = [mm(inverse[2 * u], targets[u][:tokens]) for u in both]
        second = [targets[u][tokens:] - mm(system[u][1], first[u]) for u in both]
        second = [mm(inverse[2 * u + 1], second[u]) for u in both]
        solved = [jnp.concatenate([first[u], second[u]], axis=0) for u in both]
        readers = []
        for u in both:
            mixing = jnp.exp(one_j(run_col[u]) - run_row[u] + bias_m_ref[...])
            mixing = mixing * products[u][steps : steps + tokens]
            to_end = jnp.exp(run_last[u] - run_row[u] + rows_ref[0, 0:1, :])
            readers.append(
                jnp.concatenate([to_end * products[u][steps + tokens :], mixing], axis=0)
            )
        gathered = [mm_wide(readers[u], solved[u]) for u in both]
        for u in both:
            through = jnp.exp(run_last[u] + rows_ref[1, 0:1, :width])
            transit = through * eye_width - gathered[u][:width, width:]
            correction = one_j(opened[u]) * query[u].astype(F32) - gathered[u][width:, width:]
            maps_ref[ids[u]] = jnp.concatenate([transit, correction], axis=0).astype(BF)
            terms_ref[ids[u]] = gathered[u][:, :width]

    def chain(pair):
        for u in both:
            head = pair * GROUP + u

            @pl.when(has_left)
            def _():
                state_copy(head).wait_recv()

            result = terms_ref[head] + mm(maps_ref[head], arrived_ref[head])

            @pl.when(has_right)
            def _():
                leaving_ref[head] = result[:width].astype(BF)
                state_copy(head).start()

            out_ref[head] = result[width:].astype(BF)

    def turn(step, carry):
        @pl.when(step < pairs)
        def _():
            @pl.when(has_left)
            def _():
                for copy in border_copies(step):
                    copy.wait_recv()

            local(step)

        ready = step - me

        @pl.when((ready >= 0) & (ready < pairs))
        def _():
            chain(ready)

        return carry

    lax.fori_loop(0, pairs + n_seq - 1, turn, 0)

    @pl.when(has_right)
    def _():
        def finish(pair, carry):
            for copy in border_copies(pair):
                copy.wait_send()
            for u in both:
                state_copy(pair * GROUP + u).wait_send()
            return carry

        lax.fori_loop(0, pairs, finish, 0)


def body(
    queries,
    key_pairs,
    value_pairs,
    strengths,
    decays,
    conv_query,
    conv_key,
    conv_value,
    doc_lengths,
):
    heads, tokens, width = queries.shape
    n_seq = lax.axis_size("seq")
    steps = 2 * tokens
    pairs = heads // GROUP
    vmem = pl.BlockSpec(memory_space=pltpu.VMEM)
    return pl.pallas_call(
        functools.partial(kernel, n_seq),
        out_shape=jax.ShapeDtypeStruct((heads, tokens, width), BF),
        in_specs=[pl.BlockSpec(memory_space=pltpu.SMEM)] + [vmem] * 8,
        out_specs=vmem,
        scratch_shapes=[
            pltpu.VMEM((heads, 16, width), BF),
            pltpu.VMEM((heads, 16, 2 * width), BF),
            pltpu.VMEM((heads, 16, 2 * width), BF),
            pltpu.VMEM((GROUP, 16 + tokens, 5 * width), F32),
            pltpu.VMEM((3, tokens, tokens), F32),
            pltpu.VMEM((steps, steps), F32),
            pltpu.VMEM((tokens, steps), F32),
            pltpu.VMEM((steps, tokens), F32),
            pltpu.VMEM((2, 8, steps), F32),
            pltpu.VMEM((steps, heads), F32),
            pltpu.VMEM((steps, heads), F32),
            pltpu.VMEM((heads, steps), F32),
            pltpu.VMEM((heads, 2 * width, width), BF),
            pltpu.VMEM((heads, 2 * width, width), F32),
            pltpu.VMEM((heads, width, width), BF),
            pltpu.VMEM((heads, width, width), BF),
            pltpu.SemaphoreType.DMA((3, pairs)),
            pltpu.SemaphoreType.DMA((3, pairs)),
            pltpu.SemaphoreType.DMA((heads,)),
            pltpu.SemaphoreType.DMA((heads,)),
        ],
        compiler_params=pltpu.CompilerParams(
            collective_id=0, has_side_effects=True, vmem_limit_bytes=48 << 20
        ),
        name="delta_product",
    )(
        doc_lengths,
        queries,
        key_pairs,
        value_pairs,
        strengths,
        decays,
        conv_query,
        conv_key,
        conv_value,
    )


def solution(mesh):
    in_specs = (
        P(None, ("dp", "seq"), None),
        P(None, ("dp", "seq"), None),
        P(None, ("dp", "seq"), None),
        P(None, ("dp", "seq")),
        P(None, ("dp", "seq")),
        P(),
        P(),
        P(),
        P("dp"),
    )
    out_specs = P(None, ("dp", "seq"), None)
    return jax.shard_map(body, mesh=mesh, in_specs=in_specs, out_specs=out_specs, check_vma=False)
```

time: 890 us -> 51.3 us (0.06)
  other arithmetic: 428 us -> 0 us
  local copies, waits for them, and re-layouts: 181 us -> 8.79 us
  waiting for transfers between devices: 149 us -> 0 us
  matrix products: 106 us -> 0 us
  Pallas kernels: 0 us -> 42 us
  between operations: 13.6 us -> 0.02 us
    another operation x145 -> x0, other arithmetic: 329 us -> none  [the longest x48 315 us: head_terms(): jax.scipy.linalg.solve_triangular(system, targets, lower=True, unit_diago...]
    all_gather x1 -> x0, waiting for transfers between devices: 149 us -> none  [entering(): gathered = lax.all_gather(part, axis)]
    dot_general x72 -> x0, matrix products: 92.1 us -> none  [the longest x7 24.5 us: compose(): jnp.einsum('hij,hjk->hik', early, late[:, :key_width], precision=highest,...]
    another operation x306 -> x0, local copies, waits for them, and re-layouts: 82.4 us -> none
    dynamic_slice x30 -> x0, local copies, waits for them, and re-layouts: 46.6 us -> none  [the longest x14 35.4 us: one(): return combine(state, lax.dynamic_index_in_dim(gathered, hop, 0, False))]
    pallas_call x0 -> x1, Pallas kernels: none -> 42 us  [body(): pl.pallas_call(functools.partial(kernel, n_seq), out_shape=jax.ShapeDtype...]
    slice x72 -> x0, local copies, waits for them, and re-layouts: 39.3 us -> none  [the longest x16 10.6 us: head_terms(): open_gain[steps - 1] * jnp.eye(key_width, dtype=jnp.float32)]
    select_n x16 -> x0, other arithmetic: 21.2 us -> none  [head_terms(): jnp.where(segment == segment[steps - 1], jnp.exp(running[steps - 1] - run...]
  transfers between devices with their start and end apart: 2 -> 0, of which waited for: 1 -> 0; matrix products, arithmetic and copies ran while one was open for 1% -> 0% of each run, Pallas kernels for 0% -> 0%
where the time goes in v1:
time: 51.3 us; the launch traced here: 50.8 us
  Pallas kernels  42 us (82%)
  local copies, waits for them, and re-layouts  8.79 us (17%)
    pallas_call x1, Pallas kernels, body(): pl.pallas_call(functools.partial(kernel, n_seq), out_shape=jax.ShapeDtype...  42 us
    unnamed x19, local copies, waits for them, and re-layouts  8.79 us

profile of v1, /device:TPU:27, one launch (start us, length us, event | category | flops | bytes accessed | tf_op | source)
XLA Modules:
  0.0 50.8 jit_solution(5779420185335235564)
XLA Ops:
  0.0 0.0 copy-start
  0.0 1.2 %copy-done = bf16[16,128,256]{2,1,0:T(8,128)(2,1)S(1)} copy-done((bf16[16,128,256]{2,1,0:T(8,128)(2,1)S(1)}, bf16[16,128,256]{2,1,0:T(8,128)(2,1)}, u32[]{:S(2)}) %copy-start) | copy-done | bytes 1048600
  1.2 0.0 copy-start.1
  1.2 1.2 %copy-done.1 = bf16[16,128,256]{2,1,0:T(8,128)(2,1)S(1)} copy-done((bf16[16,128,256]{2,1,0:T(8,128)(2,1)S(1)}, bf16[16,128,256]{2,1,0:T(8,128)(2,1)}, u32[]{:S(2)}) %copy-start.1) | copy-done | bytes 1048600
  2.5 0.0 copy-start.2
  2.5 1.0 %copy-done.2 = bf16[16,128,128]{2,1,0:T(8,128)(2,1)S(1)} copy-done((bf16[16,128,128]{2,1,0:T(8,128)(2,1)S(1)}, bf16[16,128,128]{2,1,0:T(8,128)(2,1)}, u32[]{:S(2)}) %copy-start.2) | copy-done | bytes 524312
  3.5 0.0 copy-start.3
  3.5 0.8 %copy-done.3 = f32[16,4,256]{2,1,0:T(4,128)S(1)} copy-done((f32[16,4,256]{2,1,0:T(4,128)S(1)}, f32[16,4,256]{2,1,0:T(4,128)}, u32[]{:S(2)}) %copy-start.3) | copy-done | bytes 65560
  4.3 0.0 copy-start.4
  4.3 0.8 %copy-done.4 = f32[16,4,256]{2,1,0:T(4,128)S(1)} copy-done((f32[16,4,256]{2,1,0:T(4,128)S(1)}, f32[16,4,256]{2,1,0:T(4,128)}, u32[]{:S(2)}) %copy-start.4) | copy-done | bytes 65560
  5.2 0.0 copy-start.5
  5.2 0.8 %copy-done.5 = f32[16,4,128]{2,1,0:T(4,128)S(1)} copy-done((f32[16,4,128]{2,1,0:T(4,128)S(1)}, f32[16,4,128]{2,1,0:T(4,128)}, u32[]{:S(2)}) %copy-start.5) | copy-done | bytes 32792
  5.9 0.0 copy-start.6
  5.9 0.7 %copy-done.6 = f32[16,256]{1,0:T(8,128)S(1)} copy-done((f32[16,256]{1,0:T(8,128)S(1)}, f32[16,256]{1,0:T(8,128)}, u32[]{:S(2)}) %copy-start.6) | copy-done | bytes 16408
  6.6 0.0 copy-start.7
  6.7 0.7 %copy-done.7 = f32[16,128]{1,0:T(8,128)S(1)} copy-done((f32[16,128]{1,0:T(8,128)S(1)}, f32[16,128]{1,0:T(8,128)}, u32[]{:S(2)}) %copy-start.7) | copy-done | bytes 8216
  7.3 0.0 copy-start.8
  7.3 0.7 %copy-done.8 = s32[8]{0:T(128)S(1)} copy-done((s32[8]{0:T(128)S(1)}, s32[8]{0:T(128)}, u32[]{:S(2)}) %copy-start.8) | copy-done | bytes 56
  8.0 42.0 %delta_product.1 = bf16[16,128,128]{2,1,0:T(8,128)(2,1)S(1)} custom-call(s32[8]{0:T(128)S(1)} %copy-done.8, bf16[16,128,128]{2,1,0:T(8,128)(2,1)S(1)} %copy-done.2, bf16[16,128,256]{2,1,0:T(8,128)(2,1)S(1)} %copy-done, bf16[16,128,256]{2,1,0:T(8,128)(2,1)S(1)} %copy-done.1, f32[16,256]{1,0:T(8,128)S(1)} %copy-done.6, f32[16,128]{1,0:T(8,128)S(1)} %copy-done.7, ...), custom_call_target="tpu_custom_call" | custom-call | tf_op jit(solution)/shard_map/delta_product/pallas_call | solution.py:373
  50.0 0.8 %copy.11 = bf16[16,128,128]{2,1,0:T(8,128)(2,1)} copy(bf16[16,128,128]{2,1,0:T(8,128)(2,1)S(1)} %delta_product.1) | data formatting | bytes 1048576
Async XLA Ops:
  0.0 1.2 %copy-start = (bf16[16,128,256]{2,1,0:T(8,128)(2,1)S(1)}, bf16[16,128,256]{2,1,0:T(8,128)(2,1)}, u32[]{:S(2)}) copy-start(bf16[16,128,256]{2,1,0:T(8,128)(2,1)} %k_ref.1) | copy-start | bytes 3145732
  1.2 1.2 %copy-start.1 = (bf16[16,128,256]{2,1,0:T(8,128)(2,1)S(1)}, bf16[16,128,256]{2,1,0:T(8,128)(2,1)}, u32[]{:S(2)}) copy-start(bf16[16,128,256]{2,1,0:T(8,128)(2,1)} %v_ref.1) | copy-start | bytes 3145732
  2.5 1.0 %copy-start.2 = (bf16[16,128,128]{2,1,0:T(8,128)(2,1)S(1)}, bf16[16,128,128]{2,1,0:T(8,128)(2,1)}, u32[]{:S(2)}) copy-start(bf16[16,128,128]{2,1,0:T(8,128)(2,1)} %q_ref.1) | copy-start | bytes 1572868
  3.5 0.8 %copy-start.3 = (f32[16,4,256]{2,1,0:T(4,128)S(1)}, f32[16,4,256]{2,1,0:T(4,128)}, u32[]{:S(2)}) copy-start(f32[16,4,256]{2,1,0:T(4,128)} %ck_ref.1) | copy-start | bytes 196612
  4.3 0.8 %copy-start.4 = (f32[16,4,256]{2,1,0:T(4,128)S(1)}, f32[16,4,256]{2,1,0:T(4,128)}, u32[]{:S(2)}) copy-start(f32[16,4,256]{2,1,0:T(4,128)} %cv_ref.1) | copy-start | bytes 196612
  5.2 0.8 %copy-start.5 = (f32[16,4,128]{2,1,0:T(4,128)S(1)}, f32[16,4,128]{2,1,0:T(4,128)}, u32[]{:S(2)}) copy-start(f32[16,4,128]{2,1,0:T(4,128)} %cq_ref.1) | copy-start | bytes 98308
  5.9 0.7 %copy-start.6 = (f32[16,256]{1,0:T(8,128)S(1)}, f32[16,256]{1,0:T(8,128)}, u32[]{:S(2)}) copy-start(f32[16,256]{1,0:T(8,128)} %strength_ref.1) | copy-start | bytes 49156
  6.6 0.7 %copy-start.7 = (f32[16,128]{1,0:T(8,128)S(1)}, f32[16,128]{1,0:T(8,128)}, u32[]{:S(2)}) copy-start(f32[16,128]{1,0:T(8,128)} %decay_ref.1) | copy-start | bytes 24580
  7.3 0.7 %copy-start.8 = (s32[8]{0:T(128)S(1)}, s32[8]{0:T(128)}, u32[]{:S(2)}) copy-start(s32[8]{0:T(128)} %docs_ref.1) | copy-start | bytes 100

commit v2 on v1

--- a/solution.py
+++ b/solution.py
@@ -11,7 +11,8 @@
 BF = jnp.bfloat16
 F32 = jnp.float32
 FAR = -1e30
-GROUP = 2
+GROUP = 8
+PART = 4
 NT = (((1,), (1,)), ((), ()))
 
 
@@ -42,6 +43,16 @@
 
 def kernel(
     n_seq,
+    docs_hbm,
+    q_hbm,
+    k_hbm,
+    v_hbm,
+    strength_hbm,
+    decay_hbm,
+    cq_hbm,
+    ck_hbm,
+    cv_hbm,
+    out_ref,
     docs_ref,
     q_ref,
     k_ref,
@@ -51,7 +62,6 @@
     cq_ref,
     ck_ref,
     cv_ref,
-    out_ref,
     bq_ref,
     bk_ref,
     bv_ref,
@@ -64,44 +74,103 @@
     beta_cols_ref,
     run_cols_ref,
     run_rows_ref,
-    maps_ref,
+    keys_ref,
+    solved_ref,
     terms_ref,
+    transit_ref,
+    local_ref,
+    correction_ref,
     arrived_ref,
     leaving_ref,
+    pair_in_ref,
+    pair_out_ref,
+    load_sem,
     border_send,
     border_recv,
+    pair_send,
+    pair_recv,
     state_send,
     state_recv,
+    back_send,
+    back_recv,
 ):
     heads, tokens, width = q_ref.shape
     half = tokens // 2
     steps = 2 * tokens
-    pairs = heads // GROUP
+    parts = heads // PART
     me = lax.axis_index("seq")
+    chip = me // 2
+    chips = n_seq // 2
+    upper = me % 2 == 1
+    lower = me % 2 == 0
     offset = me * tokens
     has_left = me > 0
     has_right = me < n_seq - 1
+    passes_on = upper & has_right
     barrier = pltpu.get_barrier_semaphore()
 
     @pl.when(has_left)
     def _():
         pl.semaphore_signal(barrier, inc=1, device_id={"seq": me - 1}, device_id_type=MESH)
 
-    def border_copies(pair):
-        span = pl.ds(pair * GROUP, GROUP)
+    @pl.when(upper & (chip > 0))
+    def _():
+        pl.semaphore_signal(barrier, inc=1, device_id={"seq": me - 2}, device_id_type=MESH)
+
+    @pl.when(lower)
+    def _():
+        pl.semaphore_signal(barrier, inc=1, device_id={"seq": me + 1}, device_id_type=MESH)
+
+    spans = [pl.ds(0, GROUP), pl.ds(GROUP, heads - GROUP)]
+    wide = [(q_hbm, q_ref), (k_hbm, k_ref), (v_hbm, v_ref)]
+    small = [
+        (docs_hbm, docs_ref),
+        (decay_hbm, decay_ref),
+        (strength_hbm, strength_ref),
+        (cq_hbm, cq_ref),
+        (ck_hbm, ck_ref),
+        (cv_hbm, cv_ref),
+    ]
+    small_loads = [
+        pltpu.make_async_copy(source, target, load_sem.at[i])
+        for i, (source, target) in enumerate(small)
+    ]
+    wide_loads = [
+        [
+            pltpu.make_async_copy(
+                source.at[span], target.at[span], load_sem.at[len(small) + 3 * part + i]
+            )
+            for i, (source, target) in enumerate(wide)
+        ]
+        for part, span in enumerate(spans)
+    ]
+    for copy in small_loads + wide_loads[0] + wide_loads[1]:
+        copy.start()
+
+    def border_copies(part):
         return [
             pltpu.make_async_remote_copy(
-                src_ref=source.at[span, pl.ds(tokens - 16, 16), :],
-                dst_ref=target.at[span],
-                send_sem=border_send.at[which, pair],
-                recv_sem=border_recv.at[which, pair],
+                src_ref=source.at[spans[part], pl.ds(tokens - 16, 16), :],
+                dst_ref=target.at[spans[part]],
+                send_sem=border_send.at[which, part],
+                recv_sem=border_recv.at[which, part],
                 device_id={"seq": me + 1},
                 device_id_type=MESH,
             )
             for which, (source, target) in enumerate(
-                [(q_ref, bq_ref), (k_ref, bk_ref), (v_ref, bv_ref)]
-            )
-        ]
+                [(q_hbm, bq_ref), (k_hbm, bk_ref), (v_hbm, bv_ref)]
+            )
+        ]
+
+    def pair_copy(head):
+        return pltpu.make_async_remote_copy(
+            src_ref=pair_out_ref.at[head],
+            dst_ref=pair_in_ref.at[head],
+            send_sem=pair_send.at[head],
+            recv_sem=pair_recv.at[head],
+            device_id={"seq": me + 1},
+            device_id_type=MESH,
+        )
 
     def state_copy(head):
         return pltpu.make_async_remote_copy(
@@ -109,27 +178,51 @@
             dst_ref=arrived_ref.at[head],
             send_sem=state_send.at[head],
             recv_sem=state_recv.at[head],
-            device_id={"seq": me + 1},
+            device_id={"seq": me + 2},
             device_id_type=MESH,
         )
 
-    @pl.when(has_right)
+    def back_copy(head):
+        return pltpu.make_async_remote_copy(
+            src_ref=arrived_ref.at[head],
+            dst_ref=arrived_ref.at[head],
+            send_sem=back_send.at[head],
+            recv_sem=back_recv.at[head],
+            device_id={"seq": me - 1},
+            device_id_type=MESH,
+        )
+
+    def send_borders():
+        for part in range(2):
+            for copy in border_copies(part):
+                copy.start()
+
+    @pl.when(lower)
     def _():
         pl.semaphore_wait(barrier, 1)
-
-        def send(pair, carry):
-            for copy in border_copies(pair):
-                copy.start()
-            return carry
-
-        lax.fori_loop(0, pairs, send, 0)
+        send_borders()
+
+    @pl.when(passes_on)
+    def _():
+        pl.semaphore_wait(barrier, 3)
+        send_borders()
+
+    @pl.when(me == n_seq - 1)
+    def _():
+        pl.semaphore_wait(barrier, 1)
 
     @pl.when(me == 0)
     def _():
         bq_ref[...] = jnp.zeros_like(bq_ref)
         bk_ref[...] = jnp.zeros_like(bk_ref)
         bv_ref[...] = jnp.zeros_like(bv_ref)
+
+    @pl.when(chip == 0)
+    def _():
         arrived_ref[...] = jnp.zeros_like(arrived_ref)
+
+    for copy in small_loads:
+        copy.wait()
 
     def token_of(index):
         return (index // tokens) * half + index % half
@@ -210,13 +303,10 @@
         ids = [pair * GROUP + u for u in both]
         for u in both:
             head = ids[u]
-            ext_ref[u, 0:16, 0:width] = bq_ref[head].astype(F32)
             ext_ref[u, 0:16, width : 3 * width] = bk_ref[head].astype(F32)
             ext_ref[u, 0:16, 3 * width : 5 * width] = bv_ref[head].astype(F32)
-            ext_ref[u, 16 : 16 + tokens, 0:width] = q_ref[head].astype(F32)
             ext_ref[u, 16 : 16 + tokens, width : 3 * width] = k_ref[head].astype(F32)
             ext_ref[u, 16 : 16 + tokens, 3 * width : 5 * width] = v_ref[head].astype(F32)
-        query = [unit(convolved(u, ids[u], 0, cq_ref, 0)) for u in both]
         keys = [
             arranged(
                 unit(convolved(u, ids[u], width, ck_ref, 0)),
@@ -248,7 +338,7 @@
         ]
         products = [
             lax.dot_general(
-                jnp.concatenate([keys[u], query[u], eye_width.astype(BF)], axis=0),
+                jnp.concatenate([keys[u], eye_width.astype(BF)], axis=0),
                 keys[u],
                 NT,
                 preferred_element_type=F32,
@@ -289,69 +379,186 @@
         second = [targets[u][tokens:] - mm(system[u][1], first[u]) for u in both]
         second = [mm(inverse[2 * u + 1], second[u]) for u in both]
         solved = [jnp.concatenate([first[u], second[u]], axis=0) for u in both]
-        readers = []
-        for u in both:
-            mixing = jnp.exp(one_j(run_col[u]) - run_row[u] + bias_m_ref[...])
-            mixing = mixing * products[u][steps : steps + tokens]
-            to_end = jnp.exp(run_last[u] - run_row[u] + rows_ref[0, 0:1, :])
-            readers.append(
-                jnp.concatenate([to_end * products[u][steps + tokens :], mixing], axis=0)
-            )
-        gathered = [mm_wide(readers[u], solved[u]) for u in both]
+        to_end = [
+            (jnp.exp(run_last[u] - run_row[u] + rows_ref[0, 0:1, :]) * products[u][steps:]).astype(BF)
+            for u in both
+        ]
+        moved = [mm(to_end[u], solved[u]) for u in both]
         for u in both:
             through = jnp.exp(run_last[u] + rows_ref[1, 0:1, :width])
-            transit = through * eye_width - gathered[u][:width, width:]
-            correction = one_j(opened[u]) * query[u].astype(F32) - gathered[u][width:, width:]
-            maps_ref[ids[u]] = jnp.concatenate([transit, correction], axis=0).astype(BF)
-            terms_ref[ids[u]] = gathered[u][:, :width]
-
-    def chain(pair):
-        for u in both:
-            head = pair * GROUP + u
-
-            @pl.when(has_left)
+            transit = (through * eye_width - moved[u][:, width:]).astype(BF)
+            terms_ref[ids[u]] = moved[u][:, :width]
+            transit_ref[ids[u]] = transit
+            pair_out_ref[ids[u]] = jnp.concatenate([moved[u][:, :width].astype(BF), transit], axis=1)
+            keys_ref[ids[u]] = keys[u]
+            solved_ref[ids[u]] = solved[u]
+
+    some = range(PART)
+
+    def read_local(part):
+        ids = [part * PART + u for u in some]
+        for u in some:
+            ext_ref[u, 0:16, 0:width] = bq_ref[ids[u]].astype(F32)
+            ext_ref[u, 16 : 16 + tokens, 0:width] = q_ref[ids[u]].astype(F32)
+        query = [unit(convolved(u, ids[u], 0, cq_ref, 0)) for u in some]
+        run_col = [
+            jnp.sum(
+                jnp.where(lane_head[:tokens] == ids[u], one_j(run_cols_ref[...]), 0.0),
+                axis=1,
+                keepdims=True,
+            )
+            for u in some
+        ]
+        scores = [
+            lax.dot_general(query[u], keys_ref[ids[u]], NT, preferred_element_type=F32)
+            for u in some
+        ]
+        mixing = [
+            jnp.exp(run_col[u] - run_rows_ref[pl.ds(ids[u], 1), :] + bias_m_ref[...]) * scores[u]
+            for u in some
+        ]
+        gathered = [mm_wide(mixing[u], solved_ref[ids[u]]) for u in some]
+        for u in some:
+            opened = jnp.exp(run_col[u] + one_j(open_col_ref[...]))
+            correction = opened * query[u].astype(F32) - gathered[u][:, width:]
+            correction_ref[ids[u]] = correction.astype(BF)
+            local_ref[ids[u]] = gathered[u][:, :width]
+
+    def compose(part):
+        ids = [part * PART + u for u in some]
+        for head in ids:
+            pair_copy(head).wait_recv()
+        composed = [mm(transit_ref[head], pair_in_ref[head]) for head in ids]
+        for head, both_maps in zip(ids, composed):
+            terms_ref[head] = terms_ref[head] + both_maps[:, :width]
+            transit_ref[head] = both_maps[:, width:].astype(BF)
+
+    def chain(part):
+        ids = [part * PART + u for u in some]
+
+        @pl.when(chip > 0)
+        def _():
+            for head in ids:
+                state_copy(head).wait_recv()
+
+        @pl.when(has_right)
+        def _():
+            ends = [terms_ref[head] + mm(transit_ref[head], arrived_ref[head]) for head in ids]
+            for head, end in zip(ids, ends):
+                leaving_ref[head] = end.astype(BF)
+            for head in ids:
+                state_copy(head).start()
+
+        @pl.when(chip > 0)
+        def _():
+            for head in ids:
+                back_copy(head).start()
+
+    def read_upper(part):
+        ids = [part * PART + u for u in some]
+        inner = [
+            mm(pair_in_ref[head, :, width:], arrived_ref[head])
+            + pair_in_ref[head, :, :width].astype(F32)
+            for head in ids
+        ]
+        reads = [
+            local_ref[head] + mm(correction_ref[head], state) for head, state in zip(ids, inner)
+        ]
+        for head, rows in zip(ids, reads):
+            out_ref[head] = rows.astype(BF)
+
+    def read_lower(part):
+        ids = [part * PART + u for u in some]
+
+        @pl.when(chip > 0)
+        def _():
+            for head in ids:
+                back_copy(head).wait_recv()
+
+        reads = [local_ref[head] + mm(correction_ref[head], arrived_ref[head]) for head in ids]
+        for head, rows in zip(ids, reads):
+            out_ref[head] = rows.astype(BF)
+
+    def first_phase(step, carry):
+        for part in range(2):
+
+            @pl.when(step == part)
             def _():
-                state_copy(head).wait_recv()
-
-            result = terms_ref[head] + mm(maps_ref[head], arrived_ref[head])
-
-            @pl.when(has_right)
-            def _():
-                leaving_ref[head] = result[:width].astype(BF)
-                state_copy(head).start()
-
-            out_ref[head] = result[width:].astype(BF)
-
-    def turn(step, carry):
-        @pl.when(step < pairs)
-        def _():
-            @pl.when(has_left)
-            def _():
-                for copy in border_copies(step):
-                    copy.wait_recv()
-
-            local(step)
-
-        ready = step - me
-
-        @pl.when((ready >= 0) & (ready < pairs))
+                for copy in wide_loads[part]:
+                    copy.wait()
+
+                @pl.when(has_left)
+                def _():
+                    for copy in border_copies(part):
+                        copy.wait_recv()
+
+        local(step)
+
+        @pl.when(lower)
+        def _():
+            for u in both:
+                pair_copy(step * GROUP + u).start()
+
+        return carry
+
+    lax.fori_loop(0, heads // GROUP, first_phase, 0)
+
+    def second_phase(step, carry):
+        ready = step - chip
+
+        @pl.when(upper & (step < parts))
+        def _():
+            compose(step)
+
+        @pl.when(upper & (ready >= 0) & (ready < parts))
         def _():
             chain(ready)
 
+        @pl.when(step < parts)
+        def _():
+            read_local(step)
+
+        @pl.when(upper & (ready >= 0) & (ready < parts))
+        def _():
+            read_upper(ready)
+
+        @pl.when(lower & (ready >= 1) & (ready <= parts))
+        def _():
+            read_lower(ready - 1)
+
         return carry
 
-    lax.fori_loop(0, pairs + n_seq - 1, turn, 0)
+    lax.fori_loop(0, parts + chips, second_phase, 0)
 
     @pl.when(has_right)
     def _():
-        def finish(pair, carry):
-            for copy in border_copies(pair):
+        for part in range(2):
+            for copy in border_copies(part):
                 copy.wait_send()
-            for u in both:
-                state_copy(pair * GROUP + u).wait_send()
+
+    @pl.when(lower)
+    def _():
+        def finish(head, carry):
+            pair_copy(head).wait_send()
             return carry
 
-        lax.fori_loop(0, pairs, finish, 0)
+        lax.fori_loop(0, heads, finish, 0)
+
+    @pl.when(passes_on)
+    def _():
+        def finish(head, carry):
+            state_copy(head).wait_send()
+            return carry
+
+        lax.fori_loop(0, heads, finish, 0)
+
+    @pl.when(upper & (chip > 0))
+    def _():
+        def finish(head, carry):
+            back_copy(head).wait_send()
+            return carry
+
+        lax.fori_loop(0, heads, finish, 0)
 
 
 def body(
@@ -368,14 +575,22 @@
     heads, tokens, width = queries.shape
     n_seq = lax.axis_size("seq")
     steps = 2 * tokens
-    pairs = heads // GROUP
     vmem = pl.BlockSpec(memory_space=pltpu.VMEM)
     return pl.pallas_call(
         functools.partial(kernel, n_seq),
         out_shape=jax.ShapeDtypeStruct((heads, tokens, width), BF),
-        in_specs=[pl.BlockSpec(memory_space=pltpu.SMEM)] + [vmem] * 8,
+        in_specs=[pl.BlockSpec(memory_space=pltpu.HBM)] * 9,
         out_specs=vmem,
         scratch_shapes=[
+            pltpu.SMEM(doc_lengths.shape, jnp.int32),
+            pltpu.VMEM(queries.shape, BF),
+            pltpu.VMEM(key_pairs.shape, BF),
+            pltpu.VMEM(value_pairs.shape, BF),
+            pltpu.VMEM(strengths.shape, F32),
+            pltpu.VMEM(decays.shape, F32),
+            pltpu.VMEM(conv_query.shape, F32),
+            pltpu.VMEM(conv_key.shape, F32),
+            pltpu.VMEM(conv_value.shape, F32),
             pltpu.VMEM((heads, 16, width), BF),
             pltpu.VMEM((heads, 16, 2 * width), BF),
             pltpu.VMEM((heads, 16, 2 * width), BF),
@@ -388,17 +603,28 @@
             pltpu.VMEM((steps, heads), F32),
             pltpu.VMEM((steps, heads), F32),
             pltpu.VMEM((heads, steps), F32),
-            pltpu.VMEM((heads, 2 * width, width), BF),
-            pltpu.VMEM((heads, 2 * width, width), F32),
+            pltpu.VMEM((heads, steps, width), BF),
+            pltpu.VMEM((heads, steps, 2 * width), F32),
+            pltpu.VMEM((heads, width, width), F32),
+            pltpu.VMEM((heads, width, width), BF),
+            pltpu.VMEM((heads, tokens, width), F32),
+            pltpu.VMEM((heads, tokens, width), BF),
             pltpu.VMEM((heads, width, width), BF),
             pltpu.VMEM((heads, width, width), BF),
-            pltpu.SemaphoreType.DMA((3, pairs)),
-            pltpu.SemaphoreType.DMA((3, pairs)),
+            pltpu.VMEM((heads, width, 2 * width), BF),
+            pltpu.VMEM((heads, width, 2 * width), BF),
+            pltpu.SemaphoreType.DMA((12,)),
+            pltpu.SemaphoreType.DMA((3, 2)),
+            pltpu.SemaphoreType.DMA((3, 2)),
+            pltpu.SemaphoreType.DMA((heads,)),
+            pltpu.SemaphoreType.DMA((heads,)),
+            pltpu.SemaphoreType.DMA((heads,)),
+            pltpu.SemaphoreType.DMA((heads,)),
             pltpu.SemaphoreType.DMA((heads,)),
             pltpu.SemaphoreType.DMA((heads,)),
         ],
         compiler_params=pltpu.CompilerParams(
-            collective_id=0, has_side_effects=True, vmem_limit_bytes=48 << 20
+            collective_id=0, has_side_effects=True, vmem_limit_bytes=60 << 20
         ),
         name="delta_product",
     )(

time: 51.3 us -> 30.9 us (0.60)
  Pallas kernels: 42 us -> 28.8 us
  local copies, waits for them, and re-layouts: 8.79 us -> 1.89 us
    pallas_call x1, Pallas kernels: 42 us -> 28.8 us  [body(): pl.pallas_call(functools.partial(kernel, n_seq), out_shape=jax.ShapeDtype...]
    unnamed x19 -> x1, local copies, waits for them, and re-layouts: 8.79 us -> 1.89 us
where the time goes in v2:
time: 30.9 us; the launch traced here: 30.7 us
  Pallas kernels  28.8 us (93%)
  local copies, waits for them, and re-layouts  1.89 us (6%)
    pallas_call x1, Pallas kernels, body(): pl.pallas_call(functools.partial(kernel, n_seq), out_shape=jax.ShapeDtype...  28.8 us
    unnamed x1, local copies, waits for them, and re-layouts  1.89 us

profile of v2, /device:TPU:27, one launch (start us, length us, event | category | flops | bytes accessed | tf_op | source)
XLA Modules:
  0.0 30.7 jit_solution(14993282309388986724)
XLA Ops:
  0.0 28.8 %delta_product.1 = bf16[16,128,128]{2,1,0:T(8,128)(2,1)} custom-call(s32[8]{0:T(128)} %docs_hbm.1, bf16[16,128,128]{2,1,0:T(8,128)(2,1)} %q_hbm.1, bf16[16,128,256]{2,1,0:T(8,128)(2,1)} %k_hbm.1, bf16[16,128,256]{2,1,0:T(8,128)(2,1)} %v_hbm.1, f32[16,256]{1,0:T(8,128)} %strength_hbm.1, f32[16,128]{1,0:T(8,128)} %decay_hbm.1, f32[16,4,128]{2,1,0:T(4,128)} %cq_hbm.1, ...), custom_call_target="tpu_custom_call" | custom-call | tf_op jit(solution)/shard_map/delta_product/pallas_call | solution.py:579
  28.8 1.9 %copy.11 = bf16[16,128,128]{2,1,0:T(8,128)(2,1)} copy(bf16[16,128,128]{2,1,0:T(8,128)(2,1)} %delta_product.1) | data formatting | bytes 1048576
